TPU v7x, 32 devices: a whole 2x2x4 slice. The times are simulated.
32 devices in a mesh: grp: 16 (over z, x, core), uly: 2 (over y).
Axes of the slice: x: 2, y: 2, z: 4, core: 2. Of those that a mesh axis runs over, the one named last changes fastest.
Arguments:
- queries: bfloat16 [4096, 32, 128], P(('grp', 'uly')), may hold values from -16 to 16
- keys: bfloat16 [4096, 4, 128], P(('grp', 'uly')), may hold values from -8 to 8
- values: bfloat16 [4096, 4, 128], P(('grp', 'uly')), may hold values from -6 to 6
- output_cotangent: bfloat16 [4096, 32, 128], P(('grp', 'uly')), may hold values from -6 to 6
- block_lists: int32 [128, 1], replicated, may hold values from 0 to 127, as said below
- list_counts: int32 [128], replicated, may hold values from 0 to 1, as said below
Outputs:
- attended: bfloat16 [4096, 32, 128], P(('grp', 'uly'))
- query_grad: bfloat16 [4096, 32, 128], P(('grp', 'uly'))
- key_gradient: bfloat16 [4096, 4, 128], P(('grp', 'uly'))
- value_gradient: bfloat16 [4096, 4, 128], P(('grp', 'uly'))
Inputs may be any that keep to these rules, and one draw needn't show every extreme that they name: `block_lists`: calling an aligned run of 8 blocks a group: every entry of block b's list is a block of another group than b's, and the entries of all lists of one group, counted or not, lie in pairwise different groups. `list_counts`: some block counts all 1 entries in every draw.
All inputs are finite; a program needn't handle non-finite values.
Results may differ from a plain program's by a relative error of at most 0.039.
Values may be sent and summed in bfloat16 or wider, within the bound.
No kernel may reach another device: no remote copies, remote signals or barrier semaphores. Data moves between devices by JAX's collectives and lax.ppermute only.
A program may use at most 128 MiB of HBM per device.

v0:
```python
import jax
import jax.numpy as jnp
from jax import lax
from jax.sharding import PartitionSpec as P


def on_device(queries, keys, values, output_cotangent, block_lists, list_counts):
    uly_count = lax.axis_size("uly")
    grp_count = lax.axis_size("grp")
    my_group = lax.axis_index("grp")
    tokens, head_count, head_width = queries.shape
    kv_heads = keys.shape[1]
    copies = max(1, uly_count // kv_heads)
    blocks_all, remote = block_lists.shape
    per_group = blocks_all // grp_count
    block_tok = tokens * uly_count // per_group
    group_tok = tokens * uly_count
    score_scale = head_width ** (-0.5)
    lists = block_lists.reshape(grp_count, per_group, remote)
    counted = (jnp.arange(remote)[None, :] < list_counts[:, None]).reshape(
        grp_count, per_group, remote
    )
    wanted = (lists // per_group == my_group) & counted
    send_place = jnp.sum(jnp.where(wanted, lists % per_group, 0), axis=(1, 2))
    sending = jnp.any(wanted, axis=(1, 2))
    mine_source = lax.dynamic_index_in_dim(lists, my_group, 0, keepdims=False) // per_group
    mine_counted = lax.dynamic_index_in_dim(counted, my_group, 0, keepdims=False)
    trip_count = jnp.max(jnp.sum(mine_counted.astype(jnp.int32), axis=1))

    def to_blocks(array_in):
        return array_in.reshape((per_group, block_tok) + array_in.shape[1:])

    keys_wide = jnp.repeat(keys, copies, axis=1)
    values_wide = jnp.repeat(values, copies, axis=1)
    query_heads, grad_heads, key_heads, value_heads = (
        lax.all_to_all(queries, "uly", split_axis=1, concat_axis=0, tiled=True),
        lax.all_to_all(output_cotangent, "uly", split_axis=1, concat_axis=0, tiled=True),
        lax.all_to_all(keys_wide, "uly", split_axis=1, concat_axis=0, tiled=True),
        lax.all_to_all(values_wide, "uly", split_axis=1, concat_axis=0, tiled=True),
    )
    stacked = jnp.stack([to_blocks(key_heads), to_blocks(value_heads)])
    outgoing = jnp.take(stacked, send_place, axis=1)
    arrived = lax.all_to_all(outgoing, "grp", split_axis=1, concat_axis=1, tiled=True)
    kv_local = key_heads.shape[1]
    heads_local = query_heads.shape[1]
    heads_per_group = heads_local // kv_local
    query_blk = query_heads.reshape(per_group, block_tok, kv_local, heads_per_group, head_width)
    grad_blk = grad_heads.reshape(per_group, block_tok, kv_local, heads_per_group, head_width)
    key_blk = to_blocks(key_heads)
    value_blk = to_blocks(value_heads)
    far_keys = arrived[0]
    far_values = arrived[1]
    causal = jnp.arange(block_tok)[:, None] >= jnp.arange(block_tok)[None, :]

    def logits(key_rows):
        return (
            jnp.einsum("pqkgd,pjkd->pkgqj", query_blk, key_rows, preferred_element_type=jnp.float32)
            * score_scale
        )

    def slot_rows(slot_index):
        source = lax.dynamic_index_in_dim(mine_source, slot_index, 1, keepdims=False)
        counted_slot = lax.dynamic_index_in_dim(mine_counted, slot_index, 1, keepdims=False)
        return (
            jnp.take(far_keys, source, axis=0),
            jnp.take(far_values, source, axis=0),
            counted_slot,
            source,
        )

    def masked(scores, counted_slot):
        return jnp.where(counted_slot[:, None, None, None, None], scores, -jnp.inf)

    near_scores = jnp.where(causal, logits(key_blk), -jnp.inf)
    highest = jnp.max(near_scores, axis=-1)
    denominator = jnp.sum(jnp.exp(near_scores - highest[..., None]), axis=-1)

    def max_sweep(slot_index, state_pair):
        highest, denominator = state_pair
        key_rows, value_rows, counted_slot, source = slot_rows(slot_index)
        scores = masked(logits(key_rows), counted_slot)
        new_highest = jnp.maximum(highest, jnp.max(scores, axis=-1))
        denominator = denominator * jnp.exp(highest - new_highest) + jnp.sum(
            jnp.exp(scores - new_highest[..., None]), axis=-1
        )
        return (new_highest, denominator)

    highest, denominator = lax.fori_loop(0, trip_count, max_sweep, (highest, denominator))
    log_total = highest + jnp.log(denominator)

    def softmax_weights(scores):
        return jnp.exp(scores - log_total[..., None])

    summed = jnp.einsum(
        "pkgqj,pjkd->pqkgd",
        softmax_weights(near_scores).astype(jnp.bfloat16),
        value_blk,
        preferred_element_type=jnp.float32,
    )

    def value_sweep(slot_index, summed):
        key_rows, value_rows, counted_slot, source = slot_rows(slot_index)
        weights = softmax_weights(masked(logits(key_rows), counted_slot)).astype(jnp.bfloat16)
        return summed + jnp.einsum(
            "pkgqj,pjkd->pqkgd", weights, value_rows, preferred_element_type=jnp.float32
        )

    summed = lax.fori_loop(0, trip_count, value_sweep, summed)
    attended_blk = summed.astype(jnp.bfloat16)
    row_delta = jnp.transpose(
        jnp.sum(grad_blk.astype(jnp.float32) * attended_blk.astype(jnp.float32), axis=-1),
        (0, 2, 3, 1),
    )

    def backward(scores, key_rows, value_rows):
        probs = softmax_weights(scores)
        weights = probs.astype(jnp.bfloat16)
        dprobs = jnp.einsum(
            "pqkgd,pjkd->pkgqj", grad_blk, value_rows, preferred_element_type=jnp.float32
        )
        dscores = (probs * (dprobs - row_delta[..., None])).astype(jnp.bfloat16)
        query_term = jnp.einsum(
            "pkgqj,pjkd->pqkgd", dscores, key_rows, preferred_element_type=jnp.float32
        )
        key_term = (
            jnp.einsum("pkgqj,pqkgd->pjkd", dscores, query_blk, preferred_element_type=jnp.float32)
            * score_scale
        )
        value_term = jnp.einsum(
            "pkgqj,pqkgd->pjkd", weights, grad_blk, preferred_element_type=jnp.float32
        )
        return (query_term, key_term, value_term)

    query_sum, key_near, value_near = backward(near_scores, key_blk, value_blk)
    far_grads = jnp.zeros((2, grp_count, block_tok, kv_local, head_width), jnp.float32)

    def grad_sweep(slot_index, state_pair):
        query_sum, far_grads = state_pair
        key_rows, value_rows, counted_slot, source = slot_rows(slot_index)
        query_term, key_term, value_term = backward(
            masked(logits(key_rows), counted_slot), key_rows, value_rows
        )
        routing = (
            (source[:, None] == jnp.arange(grp_count)[None, :]) & counted_slot[:, None]
        ).astype(jnp.float32)
        routed = jnp.einsum(
            "ps,xpjkd->xsjkd",
            routing,
            jnp.stack([key_term, value_term]),
            precision=lax.Precision.HIGHEST,
        )
        return (query_sum + query_term, far_grads + routed)

    query_sum, far_grads = lax.fori_loop(0, trip_count, grad_sweep, (query_sum, far_grads))
    owners = ((send_place[:, None] == jnp.arange(per_group)[None, :]) & sending[:, None]).astype(
        jnp.float32
    )
    returned = lax.all_to_all(far_grads, "grp", split_axis=1, concat_axis=1, tiled=True)
    landed = jnp.einsum("sp,xsjkd->xpjkd", owners, returned, precision=lax.Precision.HIGHEST)
    key_local = (key_near + landed[0]).reshape(group_tok, kv_local, head_width)
    value_local = (value_near + landed[1]).reshape(group_tok, kv_local, head_width)
    attended_rows = attended_blk.reshape(group_tok, heads_local, head_width)
    query_rows = (
        (query_sum * score_scale).astype(jnp.bfloat16).reshape(group_tok, heads_local, head_width)
    )
    attended, query_grad = (
        lax.all_to_all(attended_rows, "uly", split_axis=0, concat_axis=1, tiled=True),
        lax.all_to_all(query_rows, "uly", split_axis=0, concat_axis=1, tiled=True),
    )
    key_parts, value_parts = (
        lax.all_to_all(key_local, "uly", split_axis=0, concat_axis=1, tiled=True),
        lax.all_to_all(value_local, "uly", split_axis=0, concat_axis=1, tiled=True),
    )
    key_gradient = jnp.sum(key_parts.reshape(tokens, kv_heads, copies, head_width), axis=2).astype(
        jnp.bfloat16
    )
    value_gradient = jnp.sum(
        value_parts.reshape(tokens, kv_heads, copies, head_width), axis=2
    ).astype(jnp.bfloat16)
    return (attended, query_grad, key_gradient, value_gradient)


def solution(mesh):
    placed = (
        P(("grp", "uly"), None, None),
        P(("grp", "uly"), None, None),
        P(("grp", "uly"), None, None),
        P(("grp", "uly"), None, None),
        P(),
        P(),
    )
    return jax.shard_map(
        on_device,
        mesh=mesh,
        in_specs=placed,
        out_specs=(
            P(("grp", "uly"), None, None),
            P(("grp", "uly"), None, None),
            P(("grp", "uly"), None, None),
            P(("grp", "uly"), None, None),
        ),
        check_vma=False,
    )
```

profile of v0, /device:TPU:0, one launch (start us, length us, event | category | flops | bytes accessed | tf_op | source)
XLA Modules:
  0.0 215.2 jit_solution(12773727700696270377)
XLA Ops:
  0.6 1.7 copy.88
  2.3 4.2 %all-to-all-start = ((bf16[128,4,128]{2,0,1:T(8,128)(2,1)}), bf16[128,4,128]{2,0,1:T(8,128)(2,1)S(1)}, u32[]{:S(2)}, u32[]{:S(2)}) async-start(bf16[128,4,128]{2,0,1:T(8,128)(2,1)} %copy.88), calls=%async_computation | async-start | bytes 262144 | tf_op jit(solution)/shard_map/all_to_all | solution.py:38
  7.1 1.3 reduce.3
  8.5 0.7 broadcast_compare_fusion
  9.2 0.6 fusion.93
  9.9 1.6 copy.96
  11.4 2.6 %copy.90 = bf16[128,32,128]{2,0,1:T(8,128)(2,1)} copy(bf16[128,32,128]{2,1,0:T(8,128)(2,1)} %param.14) | data formatting | bytes 2097152 | tf_op args[0]
  14.0 1.4 copy.108
  15.4 3.4 %all-to-all-start.2 = ((bf16[128,4,128]{2,0,1:T(8,128)(2,1)}), bf16[128,4,128]{2,0,1:T(8,128)(2,1)S(1)}, u32[]{:S(2)}, u32[]{:S(2)}) async-start(bf16[128,4,128]{2,0,1:T(8,128)(2,1)} %copy.96), calls=%async_computation.2 | async-start | bytes 262144 | tf_op jit(solution)/shard_map/all_to_all | solution.py:39
  18.9 4.4 %all-to-all-done.2 = bf16[128,4,128]{2,0,1:T(8,128)(2,1)S(1)} async-done(((bf16[128,4,128]{2,0,1:T(8,128)(2,1)}), bf16[128,4,128]{2,0,1:T(8,128)(2,1)S(1)}, u32[]{:S(2)}, u32[]{:S(2)}) %all-to-all-start.2) | async-done | bytes 131104 | tf_op jit(solution)/shard_map/all_to_all | solution.py:39
  23.4 3.6 %all-to-all-start.1 = ((bf16[128,32,128]{2,0,1:T(8,128)(2,1)}), bf16[128,32,128]{2,0,1:T(8,128)(2,1)S(1)}, u32[]{:S(2)}, u32[]{:S(2)}) async-start(bf16[128,32,128]{2,0,1:T(8,128)(2,1)} %copy.90), calls=%async_computation.1 | async-start | bytes 2097152 | tf_op jit(solution)/shard_map/all_to_all | solution.py:36
  27.0 12.9 %all-to-all-done.1 = bf16[128,32,128]{2,0,1:T(8,128)(2,1)S(1)} async-done(((bf16[128,32,128]{2,0,1:T(8,128)(2,1)}), bf16[128,32,128]{2,0,1:T(8,128)(2,1)S(1)}, u32[]{:S(2)}, u32[]{:S(2)}) %all-to-all-start.1) | async-done | bytes 1048608 | tf_op jit(solution)/shard_map/all_to_all | solution.py:36
  39.9 3.6 %all-to-all-start.5 = ((bf16[128,32,128]{2,0,1:T(8,128)(2,1)}), bf16[128,32,128]{2,0,1:T(8,128)(2,1)S(1)}, u32[]{:S(2)}, u32[]{:S(2)}) async-start(bf16[128,32,128]{2,0,1:T(8,128)(2,1)} %copy.108), calls=%async_computation.5 | async-start | bytes 2097152 | tf_op jit(solution)/shard_map/all_to_all | solution.py:37
  43.5 0.7 convert_reduce_fusion
  44.3 0.6 gather_fusion
  45.0 0.9 select_bitcast_fusion
  45.9 9.7 %all-to-all-done.5 = bf16[128,32,128]{2,0,1:T(8,128)(2,1)S(1)} async-done(((bf16[128,32,128]{2,0,1:T(8,128)(2,1)}), bf16[128,32,128]{2,0,1:T(8,128)(2,1)S(1)}, u32[]{:S(2)}, u32[]{:S(2)}) %all-to-all-start.5) | async-done | bytes 1048608 | tf_op jit(solution)/shard_map/all_to_all | solution.py:37
  55.6 5.9 %all-to-all-start.3 = ((bf16[2,16,32,2,128]{4,2,3,0,1:T(8,128)(2,1)}), bf16[2,16,32,2,128]{4,2,3,0,1:T(8,128)(2,1)}, u32[]{:S(2)}, u32[]{:S(2)}) async-start(bf16[2,16,32,2,128]{4,2,3,0,1:T(8,128)(2,1)} %select_bitcast_fusion), calls=%async_computation.3 | async-start | bytes 1048576 | tf_op jit(solution)/shard_map/all_to_all | solution.py:43
  61.6 0.7 copy.92
  62.3 2.3 %copy.110 = bf16[2,128,16,128]{3,2,1,0:T(8,128)(2,1)S(1)} copy(bf16[2,128,16,128]{3,1,2,0:T(8,128)(2,1)} %bitcast.255) | data formatting | bytes 2097152 | tf_op jit(solution)/shard_map/all_to_all | solution.py:37
  64.6 1.8 fusion.96
  66.4 1.3 copy-done.2
  67.7 1.3 exponential_reduce_fusion
  69.0 7.0 %all-to-all-done.3 = bf16[2,16,32,2,128]{4,2,3,0,1:T(8,128)(2,1)} async-done(((bf16[2,16,32,2,128]{4,2,3,0,1:T(8,128)(2,1)}), bf16[2,16,32,2,128]{4,2,3,0,1:T(8,128)(2,1)}, u32[]{:S(2)}, u32[]{:S(2)}) %all-to-all-start.3) | async-done | bytes 524320 | tf_op jit(solution)/shard_map/all_to_all | solution.py:43
  76.0 1.1 slice_bitcast_fusion.2
  78.4 1.8 fusion.57
  80.2 1.3 copy-done.8
  81.5 3.0 %copy.101 = f32[8,2,32,32,8]{3,4,2,1,0:T(8,128)} copy(f32[8,2,32,32,8]{3,2,4,1,0:T(8,128)S(1)} %fusion.57) | data formatting | bytes 1048576 | tf_op jit(solution)/shard_map/while | solution.py:88
  84.5 1.9 copy.105
  86.4 4.7 %while.43 = (s32[]{:T(128)}, f32[8,2,8,32]{3,2,1,0:T(8,128)S(1)}, f32[8,2,8,32]{3,2,1,0:T(8,128)}, s32[]{:T(128)}, pred[8,1]{0,1:T(4,128)(4,1)S(1)}, /*index=5*/f32[8,2,32,32,8]{3,4,2,1,0:T(8,128)}, s32[]{:T(128)}) while((s32[]{:T(128)}, f32[8,2,8,32]{3,2,1,0:T(8,128)S(1)}, f32[8,2,8,32]{3,2,1,0:T(8,128)}, s32[]{:T(128)}, ...), condition=%wide.region_7.9_spmd, body=%wide.region_4.8_spmd.sunk | while | flops 925698 | bytes 3489969 | solution.py:88
  87.0 2.1 bitcast_reduce_fusion.2
  91.1 0.9 log_add_fusion
  92.0 3.5 %convolution_bitcast_fusion.1 = f32[8,32,2,8,128]{4,1,3,2,0:T(8,128)} fusion(f32[8,2,8,32,32]{3,4,2,1,0:T(8,128)} %copy-done.2, f32[8,2,8,32]{3,2,1,0:T(8,128)S(1)} %log_add_fusion, bf16[8,32,2,128,1]{3,1,0,2,4:T(8,128)(2,1)} %bitcast.260), kind=kOutput, calls=%fused_computation.52 | convolution fusion | flops 33816576 | bytes 2768896 | tf_op jit(solution)/shard_map/pkgqj,pjkd->pqkgd/dot_general | solution.py:94
  95.5 4.7 %while.44 = (s32[]{:T(128)}, f32[8,32,2,8,128]{4,1,3,2,0:T(8,128)}, s32[]{:T(128)}, pred[8,1]{0,1:T(4,128)(4,1)S(1)}, f32[8,2,32,32,8]{2,3,4,1,0:T(8,128)S(1)}, ...) while((s32[]{:T(128)}, f32[8,32,2,8,128]{4,1,3,2,0:T(8,128)}, s32[]{:T(128)}, ...), condition=%wide.region_9.11_spmd, body=%wide.region_8.10_spmd.sunk | while | flops 34603008 | bytes 4866141 | solution.py:108
  96.1 3.3 %bitcast_add_fusion.6 = f32[8,32,2,8,128]{4,1,3,2,0:T(8,128)} fusion(f32[8,32,2,8,128]{4,1,3,2,0:T(8,128)} %get-tuple-element.814, f32[8,2,32,32,8]{2,3,4,1,0:T(8,128)S(1)} %get-tuple-element.825, f32[8,2,8,32]{3,2,1,0:T(8,128)S(1)} %get-tuple-element.826, pred[8]{0:T(512)(128)(4,1)S(1)} %bitcast.277, bf16[8,32,2,128]{3,1,2,0:T(8,128)(2,1)S(1)} %get-tuple-element.827), kind=kOutput, calls=%fused_computation.9.clone.1 | convolution fusion | flops 34603008 | bytes 4866056 | tf_op jit(solution)/shard_map/while/body/pkgqj,pjkd->pqkgd/dot_general | solution.py:104
  100.2 3.1 %fusion.52 = f32[8,2,32,32,8]{3,2,4,1,0:T(8,128)} fusion(bf16[8,32,2,8,128]{4,3,2,1,0:T(8,128)(2,1)S(1)} %bitcast.243, bf16[8,32,2,128]{3,1,2,0:T(8,128)(2,1)S(1)} %get-tuple-element.868), kind=kOutput, calls=%fused_computation.76 | convolution fusion | flops 33554432 | bytes 1703936 | tf_op jit(solution)/shard_map/while/body/pqkgd,pjkd->pkgqj/dot_general | solution.py:118
  103.4 3.2 %multiply_reduce_fusion = (f32[8,32,2,8]{3,2,1,0:T(2,128)}, bf16[8,32,2,8,128]{4,3,2,1,0:T(8,128)(2,1)}) fusion(bf16[8,32,2,8,128]{4,3,2,1,0:T(8,128)(2,1)S(1)} %bitcast.244, f32[8,32,2,8,128]{4,1,3,2,0:T(8,128)S(1)} %copy-done.1), kind=kLoop, calls=%fused_computation.47 | loop fusion | flops 2093056 | bytes 4210688 | tf_op jit(solution)/shard_map/reduce_sum | solution.py:111
  106.6 1.0 copy.113
  107.6 3.3 %convolution_bitcast_fusion.4 = f32[1,8,32,2,128]{4,2,3,1,0:T(8,128)} fusion(f32[8,2,32,32,8]{3,2,4,1,0:T(8,128)} %copy-done.8, f32[8,2,8,32]{3,2,1,0:T(8,128)S(1)} %get-tuple-element.866, pred[8]{0:T(512)(128)(4,1)S(1)} %get-tuple-element.627, bf16[8,32,2,8,128]{4,3,2,1,0:T(8,128)(2,1)S(1)} %bitcast.245), kind=kOutput, calls=%fused_computation.56 | convolution fusion | flops 34078720 | bytes 1851400 | tf_op jit(solution)/shard_map/while/body/pkgqj,pqkgd->pjkd/dot_general | solution.py:129
  110.9 2.8 %fusion.28 = bf16[8,2,8,32,32]{3,4,2,1,0:T(8,128)(2,1)} fusion(f32[8,2,8,32,32]{3,4,2,1,0:T(8,128)S(1)} %copy-done.3, f32[8,2,8,32]{3,2,1,0:T(8,128)S(1)} %copy.113, f32[8,2,8,32]{3,2,1,0:T(8,128)S(1)} %get-tuple-element.866, bf16[8,32,2,8,128]{4,3,2,1,0:T(8,128)(2,1)S(1)} %bitcast.246, bf16[8,32,2,128,1]{3,1,0,2,4:T(8,128)(2,1)S(1)} %bitcast.261), kind=kOutput, calls=%fused_computation.42 | convolution fusion | flops 34078720 | bytes 1998848 | tf_op jit(solution)/shard_map/pqkgd,pjkd->pkgqj/dot_general | solution.py:118
  113.7 1.0 fusion.33
  114.7 2.9 %copy.121 = f32[8,2,32,32,8]{2,3,4,1,0:T(8,128)} copy(f32[8,2,32,32,8]{3,2,4,1,0:T(8,128)} %fusion.52) | data formatting | bytes 1048576 | tf_op jit(solution)/shard_map/while | solution.py:154
  117.7 0.9 fusion.60
  118.6 1.5 copy.123
  120.1 1.8 convolution_bitcast_fusion
  122.4 6.0 %while.45 = (s32[]{:T(128)}, f32[8,32,2,8,128]{4,1,3,2,0:T(8,128)}, f32[2,16,32,2,128]{4,3,2,1,0:T(2,128)S(1)}, s32[]{:T(128)}, pred[8,1]{0,1:T(4,128)(4,1)S(1)}...) while((s32[]{:T(128)}, f32[8,32,2,8,128]{4,1,3,2,0:T(8,128)}, ...), condition=%wide.region_12.14_spmd, body=%wide.region_11.13_spmd.sunk | while | flops 35127296 | bytes 12746905 | solution.py:154
  123.1 4.1 %bitcast_add_fusion.7 = f32[8,32,2,8,128]{4,1,3,2,0:T(8,128)} fusion(f32[8,32,2,8,128]{4,1,3,2,0:T(8,128)} %get-tuple-element.842, f32[8,2,32,32,8]{2,3,4,1,0:T(8,128)} %get-tuple-element.860, f32[8,2,32,32,8]{2,3,4,1,0:T(8,128)S(1)} %get-tuple-element.858, f32[8,2,8,32]{3,2,1,0:T(8,128)S(1)} %get-tuple-element.861, ...), kind=kOutput, calls=%fused_computation.20.clone.1 | convolution fusion | flops 34865152 | bytes 5406728 | tf_op jit(solution)/shard_map/while/body/pkgqj,pjkd->pqkgd/dot_general | solution.py:122
  128.4 4.0 %fusion.29 = bf16[8,32,2,8,128]{4,3,2,1,0:T(8,128)(2,1)} fusion(f32[8,32,2,8,128]{4,1,3,2,0:T(8,128)} %get-tuple-element.466), kind=kLoop, calls=%fused_computation.45 | loop fusion | flops 1048576 | bytes 3145728 | tf_op jit(solution)/shard_map/convert_element_type | solution.py:164
  132.4 3.6 %all-to-all-start.6 = ((bf16[256,16,128]{2,1,0:T(8,128)(2,1)}), bf16[256,16,128]{2,1,0:T(8,128)(2,1)S(1)}, u32[]{:S(2)}, u32[]{:S(2)}) async-start(bf16[256,16,128]{2,1,0:T(8,128)(2,1)} %bitcast.69), calls=%async_computation.6 | async-start | bytes 2097152 | tf_op jit(solution)/shard_map/all_to_all | solution.py:168
  136.1 13.9 %all-to-all-done.6 = bf16[256,16,128]{2,1,0:T(8,128)(2,1)S(1)} async-done(((bf16[256,16,128]{2,1,0:T(8,128)(2,1)}), bf16[256,16,128]{2,1,0:T(8,128)(2,1)S(1)}, u32[]{:S(2)}, u32[]{:S(2)}) %all-to-all-start.6) | async-done | bytes 1048608 | tf_op jit(solution)/shard_map/all_to_all | solution.py:168
  150.0 29.1 %all_to_all.124 = f32[2,16,32,2,128]{4,3,2,0,1:T(2,128)} all-to-all(f32[2,16,32,2,128]{4,3,2,0,1:T(2,128)S(1)} %copy.127), channel_id=1, replica_groups=mesh['grp'=16,'uly'=2] {'grp'}, dimensions={1} | all-to-all | bytes 2097152 | tf_op jit(solution)/shard_map/all_to_all | solution.py:158
  179.1 4.9 %all-to-all-start.4 = ((bf16[256,16,128]{2,1,0:T(8,128)(2,1)}), bf16[256,16,128]{2,1,0:T(8,128)(2,1)}, u32[]{:S(2)}, u32[]{:S(2)}) async-start(bf16[256,16,128]{2,1,0:T(8,128)(2,1)} %bitcast.252), calls=%async_computation.4 | async-start | bytes 2097152 | tf_op jit(solution)/shard_map/all_to_all | solution.py:167
  184.1 2.2 %fusion.39 = f32[2,32,2,128,8]{3,4,2,1,0:T(8,128)S(1)} fusion(f32[2,16,32,2,128]{4,3,2,0,1:T(2,128)} %all_to_all.124, s32[16]{0:T(128)S(1)} %copy-done.28, pred[16]{0:T(512)(128)(4,1)S(1)} %copy-done.26), kind=kOutput, calls=%fused_computation.64 | convolution fusion | flops 25166080 | bytes 1572944 | tf_op jit(solution)/shard_map/sp,xsjkd->xpjkd/dot_general | solution.py:159
  187.3 0.8 copy.136
  188.1 10.6 %all-to-all-done.4 = bf16[256,16,128]{2,1,0:T(8,128)(2,1)} async-done(((bf16[256,16,128]{2,1,0:T(8,128)(2,1)}), bf16[256,16,128]{2,1,0:T(8,128)(2,1)}, u32[]{:S(2)}, u32[]{:S(2)}) %all-to-all-start.4) | async-done | bytes 1048608 | tf_op jit(solution)/shard_map/all_to_all | solution.py:167
  198.7 3.4 %all-to-all-start.9 = ((bf16[256,2,128]{2,1,0:T(2,128)(2,1)}), bf16[256,2,128]{2,1,0:T(2,128)(2,1)S(1)}, u32[]{:S(2)}, u32[]{:S(2)}) async-start(bf16[256,2,128]{2,1,0:T(2,128)(2,1)} %copy.136), calls=%async_computation.9 | async-start | bytes 262144 | tf_op jit(solution)/shard_map/all_to_all | solution.py:172
  202.1 2.1 fusion.36
  204.2 0.8 copy.131
  205.0 1.6 all-to-all-done.9
  206.6 3.4 %all-to-all-start.8 = ((bf16[256,2,128]{2,1,0:T(2,128)(2,1)}), bf16[256,2,128]{2,1,0:T(2,128)(2,1)S(1)}, u32[]{:S(2)}, u32[]{:S(2)}) async-start(bf16[256,2,128]{2,1,0:T(2,128)(2,1)} %copy.131), calls=%async_computation.8 | async-start | bytes 262144 | tf_op jit(solution)/shard_map/all_to_all | solution.py:171
  210.0 1.2 copy.125
  211.1 2.4 %copy.107 = bf16[128,2,16,128]{3,2,1,0:T(8,128)(2,1)} copy(bf16[128,2,16,128]{3,2,0,1:T(8,128)(2,1)} %bitcast.44) | data formatting | bytes 2097152 | tf_op jit(solution)/shard_map/all_to_all | solution.py:167
  213.5 0.8 copy.140
  214.5 0.8 copy.139
  (93 shorter events, 6.0 us)
Async XLA Ops:
  0.6 13.4 %copy-start.24 = (bf16[128,32,128]{2,1,0:T(8,128)(2,1)S(1)}, bf16[128,32,128]{2,1,0:T(8,128)(2,1)}, u32[]{:S(2)}) copy-start(bf16[128,32,128]{2,1,0:T(8,128)(2,1)} %param.17) | copy-start | bytes 3145732
  2.3 13.1 %all-to-all-start = ((bf16[128,4,128]{2,0,1:T(8,128)(2,1)}), bf16[128,4,128]{2,0,1:T(8,128)(2,1)S(1)}, u32[]{:S(2)}, u32[]{:S(2)}) async-start(bf16[128,4,128]{2,0,1:T(8,128)(2,1)} %copy.88), calls=%async_computation | async-start | bytes 262144 | tf_op jit(solution)/shard_map/all_to_all | solution.py:38
  15.4 7.9 %all-to-all-start.2 = ((bf16[128,4,128]{2,0,1:T(8,128)(2,1)}), bf16[128,4,128]{2,0,1:T(8,128)(2,1)S(1)}, u32[]{:S(2)}, u32[]{:S(2)}) async-start(bf16[128,4,128]{2,0,1:T(8,128)(2,1)} %copy.96), calls=%async_computation.2 | async-start | bytes 262144 | tf_op jit(solution)/shard_map/all_to_all | solution.py:39
  18.9 21.0 %copy-start.27 = (s32[16]{0:T(128)}, s32[16]{0:T(128)S(1)}, u32[]{:S(2)}) copy-start(s32[16]{0:T(128)S(1)} %fusion.72) | copy-start | bytes 196
  23.4 16.6 %all-to-all-start.1 = ((bf16[128,32,128]{2,0,1:T(8,128)(2,1)}), bf16[128,32,128]{2,0,1:T(8,128)(2,1)S(1)}, u32[]{:S(2)}, u32[]{:S(2)}) async-start(bf16[128,32,128]{2,0,1:T(8,128)(2,1)} %copy.90), calls=%async_computation.1 | async-start | bytes 2097152 | tf_op jit(solution)/shard_map/all_to_all | solution.py:36
  39.9 15.7 %all-to-all-start.5 = ((bf16[128,32,128]{2,0,1:T(8,128)(2,1)}), bf16[128,32,128]{2,0,1:T(8,128)(2,1)S(1)}, u32[]{:S(2)}, u32[]{:S(2)}) async-start(bf16[128,32,128]{2,0,1:T(8,128)(2,1)} %copy.108), calls=%async_computation.5 | async-start | bytes 2097152 | tf_op jit(solution)/shard_map/all_to_all | solution.py:37
  44.2 20.4 %copy-start.19 = (bf16[2,128,2,128]{3,1,0,2:T(8,128)(2,1)}, bf16[2,128,2,128]{3,1,0,2:T(8,128)(2,1)S(1)}, u32[]{:S(2)}) copy-start(bf16[2,128,2,128]{3,1,0,2:T(8,128)(2,1)S(1)} %copy.89) | copy-start | bytes 393220
  44.2 11.4 %copy-start.21 = (bf16[2,128,2,128]{3,1,0,2:T(8,128)(2,1)}, bf16[2,128,2,128]{3,1,0,2:T(8,128)(2,1)S(1)}, u32[]{:S(2)}) copy-start(bf16[2,128,2,128]{3,1,0,2:T(8,128)(2,1)S(1)} %copy.97) | copy-start | bytes 393220
  55.6 6.7 %copy-start.16 = (bf16[128,32,128]{2,0,1:T(8,128)(2,1)}, bf16[128,32,128]{2,0,1:T(8,128)(2,1)S(1)}, u32[]{:S(2)}) copy-start(bf16[128,32,128]{2,0,1:T(8,128)(2,1)S(1)} %all-to-all-done.5) | copy-start | bytes 3145732
  55.6 20.4 %all-to-all-start.3 = ((bf16[2,16,32,2,128]{4,2,3,0,1:T(8,128)(2,1)}), bf16[2,16,32,2,128]{4,2,3,0,1:T(8,128)(2,1)}, u32[]{:S(2)}, u32[]{:S(2)}) async-start(bf16[2,16,32,2,128]{4,2,3,0,1:T(8,128)(2,1)} %select_bitcast_fusion), calls=%async_computation.3 | async-start | bytes 1048576 | tf_op jit(solution)/shard_map/all_to_all | solution.py:43
  62.3 16.1 %copy-start.10 = (bf16[2,128,16,128]{3,2,1,0:T(8,128)(2,1)}, bf16[2,128,16,128]{3,2,1,0:T(8,128)(2,1)S(1)}, u32[]{:S(2)}) copy-start(bf16[2,128,16,128]{3,2,1,0:T(8,128)(2,1)S(1)} %copy.92) | copy-start | bytes 3145732
  64.6 46.3 %copy-start.6 = (bf16[2,128,16,128]{3,2,1,0:T(8,128)(2,1)}, bf16[2,128,16,128]{3,2,1,0:T(8,128)(2,1)S(1)}, u32[]{:S(2)}) copy-start(bf16[2,128,16,128]{3,2,1,0:T(8,128)(2,1)S(1)} %copy.110) | copy-start | bytes 3145732
  66.4 1.4 copy-start.2
  80.1 1.3 copy-start.8
  87.0 2.2 %copy-start = (f32[8,2,32,32,8]{3,4,2,1,0:T(8,128)S(1)}, f32[8,2,32,32,8]{3,4,2,1,0:T(8,128)}, u32[]{:S(2)}) copy-start(f32[8,2,32,32,8]{3,4,2,1,0:T(8,128)} %get-tuple-element.803) | copy-start | bytes 1572868 | tf_op jit(solution)/shard_map/while
  87.0 2.8 %copy-start.17 = (f32[8,2,8,32]{3,2,1,0:T(8,128)S(1)}, f32[8,2,8,32]{3,2,1,0:T(8,128)}, u32[]{:S(2)}) copy-start(f32[8,2,8,32]{3,2,1,0:T(8,128)} %get-tuple-element.793) | copy-start | bytes 49156 | tf_op jit(solution)/shard_map/while
  89.8 0.6 copy-start.18
  100.2 3.1 %copy-start.1 = (f32[8,32,2,8,128]{4,1,3,2,0:T(8,128)S(1)}, f32[8,32,2,8,128]{4,1,3,2,0:T(8,128)}, u32[]{:S(2)}) copy-start(f32[8,32,2,8,128]{4,1,3,2,0:T(8,128)} %get-tuple-element.465) | copy-start | bytes 6291460
  107.6 3.3 %copy-start.3 = (f32[8,2,8,32,32]{3,4,2,1,0:T(8,128)S(1)}, f32[8,2,8,32,32]{3,4,2,1,0:T(8,128)}, u32[]{:S(2)}) copy-start(f32[8,2,8,32,32]{3,4,2,1,0:T(8,128)} %copy-done.2) | copy-start | bytes 1572868
  107.6 3.3 %copy-start.22 = (bf16[2,128,2,128]{3,1,0,2:T(8,128)(2,1)S(1)}, bf16[2,128,2,128]{3,1,0,2:T(8,128)(2,1)}, u32[]{:S(2)}) copy-start(bf16[2,128,2,128]{3,1,0,2:T(8,128)(2,1)} %copy-done.21) | copy-start | bytes 393220
  107.6 6.1 %copy-start.12 = (f32[8,2,32,32,8]{3,2,4,1,0:T(8,128)S(1)}, f32[8,2,32,32,8]{3,2,4,1,0:T(8,128)}, u32[]{:S(2)}) copy-start(f32[8,2,32,32,8]{3,2,4,1,0:T(8,128)} %fusion.52) | copy-start | bytes 1572868
  110.9 2.8 %copy-start.9 = (f32[8,2,32,32,8]{3,2,4,1,0:T(8,128)S(1)}, f32[8,2,32,32,8]{3,2,4,1,0:T(8,128)}, u32[]{:S(2)}) copy-start(f32[8,2,32,32,8]{3,2,4,1,0:T(8,128)} %copy-done.8) | copy-start | bytes 1572868
  110.9 2.8 %copy-start.11 = (bf16[2,128,16,128]{3,2,1,0:T(8,128)(2,1)S(1)}, bf16[2,128,16,128]{3,2,1,0:T(8,128)(2,1)}, u32[]{:S(2)}) copy-start(bf16[2,128,16,128]{3,2,1,0:T(8,128)(2,1)} %copy-done.10) | copy-start | bytes 3145732
  114.7 2.9 %copy-start.25 = (f32[1,8,32,2,128]{4,2,3,1,0:T(8,128)S(1)}, f32[1,8,32,2,128]{4,2,3,1,0:T(8,128)}, u32[]{:S(2)}) copy-start(f32[1,8,32,2,128]{4,2,3,1,0:T(8,128)} %convolution_bitcast_fusion.4) | copy-start | bytes 786436
  117.7 2.4 %copy-start.13 = (bf16[8,2,8,32,32]{3,4,2,1,0:T(8,128)(2,1)S(1)}, bf16[8,2,8,32,32]{3,4,2,1,0:T(8,128)(2,1)}, u32[]{:S(2)}) copy-start(bf16[8,2,8,32,32]{3,4,2,1,0:T(8,128)(2,1)} %fusion.28) | copy-start | bytes 786436
  117.7 2.4 %copy-start.20 = (bf16[2,128,2,128]{3,1,0,2:T(8,128)(2,1)S(1)}, bf16[2,128,2,128]{3,1,0,2:T(8,128)(2,1)}, u32[]{:S(2)}) copy-start(bf16[2,128,2,128]{3,1,0,2:T(8,128)(2,1)} %copy-done.19) | copy-start | bytes 393220
  123.0 4.1 %copy-start.5 = (f32[2,32,2,128,16]{3,2,1,4,0:T(2,128)S(1)}, f32[2,32,2,128,16]{3,2,1,4,0:T(2,128)}, u32[]{:S(2)}) copy-start(f32[2,32,2,128,16]{3,2,1,4,0:T(2,128)} %get-tuple-element.863) | copy-start | bytes 3145732 | tf_op jit(solution)/shard_map/while
  132.4 17.6 %all-to-all-start.6 = ((bf16[256,16,128]{2,1,0:T(8,128)(2,1)}), bf16[256,16,128]{2,1,0:T(8,128)(2,1)S(1)}, u32[]{:S(2)}, u32[]{:S(2)}) async-start(bf16[256,16,128]{2,1,0:T(8,128)(2,1)} %bitcast.69), calls=%async_computation.6 | async-start | bytes 2097152 | tf_op jit(solution)/shard_map/all_to_all | solution.py:168
  136.1 48.0 %copy-start.26 = (pred[16]{0:T(512)(128)(4,1)S(1)}, pred[16]{0:T(512)(128)(4,1)}, u32[]{:S(2)}) copy-start(pred[16]{0:T(512)(128)(4,1)} %get-tuple-element.620) | copy-start | bytes 52
  136.1 48.0 %copy-start.28 = (s32[16]{0:T(128)S(1)}, s32[16]{0:T(128)}, u32[]{:S(2)}) copy-start(s32[16]{0:T(128)} %copy-done.27) | copy-start | bytes 196
  150.0 29.1 %copy-start.14 = (bf16[256,16,128]{2,1,0:T(8,128)(2,1)}, bf16[256,16,128]{2,1,0:T(8,128)(2,1)S(1)}, u32[]{:S(2)}) copy-start(bf16[256,16,128]{2,1,0:T(8,128)(2,1)S(1)} %all-to-all-done.6) | copy-start | bytes 3145732
  179.1 7.4 %copy-start.4 = (f32[8,2,8,32,32]{3,4,2,1,0:T(8,128)S(1)}, f32[8,2,8,32,32]{3,4,2,1,0:T(8,128)}, u32[]{:S(2)}) copy-start(f32[8,2,8,32,32]{3,4,2,1,0:T(8,128)} %copy-done.2) | copy-start | bytes 1572868
  179.1 7.4 %copy-start.7 = (bf16[2,128,16,128]{3,2,1,0:T(8,128)(2,1)S(1)}, bf16[2,128,16,128]{3,2,1,0:T(8,128)(2,1)}, u32[]{:S(2)}) copy-start(bf16[2,128,16,128]{3,2,1,0:T(8,128)(2,1)} %copy-done.6) | copy-start | bytes 3145732
  179.1 19.6 %all-to-all-start.4 = ((bf16[256,16,128]{2,1,0:T(8,128)(2,1)}), bf16[256,16,128]{2,1,0:T(8,128)(2,1)}, u32[]{:S(2)}, u32[]{:S(2)}) async-start(bf16[256,16,128]{2,1,0:T(8,128)(2,1)} %bitcast.252), calls=%async_computation.4 | async-start | bytes 2097152 | tf_op jit(solution)/shard_map/all_to_all | solution.py:167
  186.5 0.8 copy-start.23
  187.3 22.6 %copy-start.15 = (bf16[256,16,128]{2,1,0:T(8,128)(2,1)S(1)}, bf16[256,16,128]{2,1,0:T(8,128)(2,1)}, u32[]{:S(2)}) copy-start(bf16[256,16,128]{2,1,0:T(8,128)(2,1)} %copy-done.14) | copy-start | bytes 3145732
  198.7 7.8 %all-to-all-start.9 = ((bf16[256,2,128]{2,1,0:T(2,128)(2,1)}), bf16[256,2,128]{2,1,0:T(2,128)(2,1)S(1)}, u32[]{:S(2)}, u32[]{:S(2)}) async-start(bf16[256,2,128]{2,1,0:T(2,128)(2,1)} %copy.136), calls=%async_computation.9 | async-start | bytes 262144 | tf_op jit(solution)/shard_map/all_to_all | solution.py:172
  206.6 7.8 %all-to-all-start.8 = ((bf16[256,2,128]{2,1,0:T(2,128)(2,1)}), bf16[256,2,128]{2,1,0:T(2,128)(2,1)S(1)}, u32[]{:S(2)}, u32[]{:S(2)}) async-start(bf16[256,2,128]{2,1,0:T(2,128)(2,1)} %copy.131), calls=%async_computation.8 | async-start | bytes 262144 | tf_op jit(solution)/shard_map/all_to_all | solution.py:171
where the time goes:
time: 217 us; the launch traced here: 215 us
  waiting for transfers between devices  60.3 us (28%)
  starting transfers between devices  35.9 us (17%)
  local copies, waits for them, and re-layouts  35.3 us (16%)
  matrix products  32.2 us (15%)
  blocking collectives  29.1 us (13%)
  other arithmetic  17.1 us (8%)
  loops' own time  4.02 us (2%)
    all_to_all x1, blocking collectives, on_device(): lax.all_to_all(far_grads, 'grp', split_axis=1, concat_axis=1, tiled=True)  29.1 us
    all_to_all x1, waiting for transfers between devices, on_device(): lax.all_to_all(query_rows, 'uly', split_axis=0, concat_axis=1, tiled=True)  13.9 us
    all_to_all x1, waiting for transfers between devices, on_device(): lax.all_to_all(queries, 'uly', split_axis=1, concat_axis=0, tiled=True)  12.9 us
    unnamed x57, local copies, waits for them, and re-layouts  12.2 us
    all_to_all x1, waiting for transfers between devices, on_device(): lax.all_to_all(attended_rows, 'uly', split_axis=0, concat_axis=1, tiled=T...  10.6 us
    all_to_all x1, waiting for transfers between devices, on_device(): lax.all_to_all(output_cotangent, 'uly', split_axis=1, concat_axis=0, tile...  9.72 us
    all_to_all x1, waiting for transfers between devices, on_device(): lax.all_to_all(outgoing, 'grp', split_axis=1, concat_axis=1, tiled=True)  7.02 us
    dot_general x2, matrix products, backward(): jnp.einsum('pkgqj,pjkd->pqkgd', dscores, key_rows, preferred_element_type...  5.96 us
  transfers between devices with their start and end apart: 9, of which 8 were waited for; matrix products, arithmetic and copies ran while one was open for 13% of the time, Pallas kernels for 0%

commit v1 on v0

--- a/solution.py
+++ b/solution.py
@@ -2,6 +2,17 @@
 import jax.numpy as jnp
 from jax import lax
 from jax.sharding import PartitionSpec as P
+
+
+def split_up(shard, dim, size):
+    before, after = (shard.shape[:dim], shard.shape[dim + 1 :])
+    return jnp.moveaxis(shard.reshape(*before, size, -1, *after), dim, 0)
+
+
+def in_order(blocks, dim):
+    dims = list(blocks.shape[1:])
+    dims[dim] *= blocks.shape[0]
+    return jnp.moveaxis(blocks, 0, dim).reshape(dims)
 
 
 def on_device(queries, keys, values, output_cotangent, block_lists, list_counts):
@@ -40,7 +51,15 @@
     )
     stacked = jnp.stack([to_blocks(key_heads), to_blocks(value_heads)])
     outgoing = jnp.take(stacked, send_place, axis=1)
-    arrived = lax.all_to_all(outgoing, "grp", split_axis=1, concat_axis=1, tiled=True)
+    peers, mine = (lax.axis_size("grp"), lax.axis_index("grp"))
+    blocks = split_up(outgoing, 1, peers)
+    out = blocks
+    for step in range(1, peers):
+        target, source_2 = ((mine + step) % peers, (mine - step) % peers)
+        sent = lax.dynamic_index_in_dim(blocks, target, 0)
+        theirs = lax.ppermute(sent, "grp", [(i, (i + step) % peers) for i in range(peers)])
+        out = lax.dynamic_update_slice_in_dim(out, theirs, source_2, axis=0)
+    arrived = in_order(out, 1)
     kv_local = key_heads.shape[1]
     heads_local = query_heads.shape[1]
     heads_per_group = heads_local // kv_local

time: 217 us -> 205 us (0.945)
  waiting for transfers between devices: 60.3 us -> 34.1 us
  starting transfers between devices: 35.9 us -> 53.9 us
  other arithmetic: 17.1 us -> 14.5 us
  local copies, waits for them, and re-layouts: 35.3 us -> 33.1 us
    ppermute x0 -> x15, starting transfers between devices: none -> 23 us  [on_device(): lax.ppermute(sent, 'grp', [(i, (i + step) % peers) for i in range(peers)])]
    all_to_all x1, waiting for transfers between devices: 12.9 us -> 0.01 us  [on_device(): lax.all_to_all(queries, 'uly', split_axis=1, concat_axis=0, tiled=True)]
    all_to_all x1, waiting for transfers between devices: 9.72 us -> 0.01 us  [on_device(): lax.all_to_all(output_cotangent, 'uly', split_axis=1, concat_axis=0, tile...]
    all_to_all x1 -> x0, waiting for transfers between devices: 7.02 us -> none  [on_device(): lax.all_to_all(outgoing, 'grp', split_axis=1, concat_axis=1, tiled=True)]
    all_to_all x1 -> x0, starting transfers between devices: 5.91 us -> none  [on_device(): lax.all_to_all(outgoing, 'grp', split_axis=1, concat_axis=1, tiled=True)]
    ppermute x0 -> x15, waiting for transfers between devices: none -> 2.17 us  [on_device(): lax.ppermute(sent, 'grp', [(i, (i + step) % peers) for i in range(peers)])]
    unnamed x57 -> x53, local copies, waits for them, and re-layouts: 12.2 us -> 11.6 us
  transfers between devices with their start and end apart: 9 -> 23, of which waited for: 8 -> 8; matrix products, arithmetic and copies ran while one was open for 13% -> 21% of each run, Pallas kernels for 0% -> 0%
where the time goes in v1:
time: 205 us; the launch traced here: 203 us
  starting transfers between devices  53.9 us (26%)
  waiting for transfers between devices  34.1 us (17%)
  matrix products  33.2 us (16%)
  local copies, waits for them, and re-layouts  33.1 us (16%)
  blocking collectives  28.3 us (14%)
  other arithmetic  14.5 us (7%)
  loops' own time  4.56 us (2%)
    all_to_all x1, blocking collectives, on_device(): lax.all_to_all(far_grads, 'grp', split_axis=1, concat_axis=1, tiled=True)  28.3 us
    ppermute x15, starting transfers between devices, on_device(): lax.ppermute(sent, 'grp', [(i, (i + step) % peers) for i in range(peers)])  23 us
    all_to_all x1, waiting for transfers between devices, on_device(): lax.all_to_all(query_rows, 'uly', split_axis=0, concat_axis=1, tiled=True)  14.9 us
    unnamed x53, local copies, waits for them, and re-layouts  11.6 us
    all_to_all x1, waiting for transfers between devices, on_device(): lax.all_to_all(attended_rows, 'uly', split_axis=0, concat_axis=1, tiled=T...  10.9 us
    dot_general x2, matrix products, backward(): jnp.einsum('pkgqj,pjkd->pqkgd', dscores, key_rows, preferred_element_type...  6.01 us
    dot_general x2, matrix products, backward(): jnp.einsum('pqkgd,pjkd->pkgqj', grad_blk, value_rows, preferred_element_t...  5.95 us
    all_to_all x1, starting transfers between devices, on_device(): lax.all_to_all(attended_rows, 'uly', split_axis=0, concat_axis=1, tiled=T...  4.67 us
  transfers between devices with their start and end apart: 23, of which 8 were waited for; matrix products, arithmetic and copies ran while one was open for 21% of the time, Pallas kernels for 0%

profile of v1, /device:TPU:0, one launch (start us, length us, event | category | flops | bytes accessed | tf_op | source)
XLA Modules:
  0.0 203.3 jit_solution(1031826136042258339)
XLA Ops:
  0.7 1.7 copy.90
  2.4 4.2 %all-to-all-start = ((bf16[128,4,128]{2,0,1:T(8,128)(2,1)}), bf16[128,4,128]{2,0,1:T(8,128)(2,1)S(1)}, u32[]{:S(2)}, u32[]{:S(2)}) async-start(bf16[128,4,128]{2,0,1:T(8,128)(2,1)} %copy.90), calls=%async_computation | async-start | bytes 262144 | tf_op jit(solution)/shard_map/all_to_all | solution.py:49
  7.1 1.3 reduce.3
  9.9 1.6 copy.98
  11.5 1.4 copy.92
  12.9 1.4 copy.110
  14.3 0.7 convert_reduce_fusion
  15.0 3.6 %all-to-all-start.2 = ((bf16[128,4,128]{2,0,1:T(8,128)(2,1)}), bf16[128,4,128]{2,0,1:T(8,128)(2,1)S(1)}, u32[]{:S(2)}, u32[]{:S(2)}) async-start(bf16[128,4,128]{2,0,1:T(8,128)(2,1)} %copy.98), calls=%async_computation.2 | async-start | bytes 262144 | tf_op jit(solution)/shard_map/all_to_all | solution.py:50
  18.6 4.5 %all-to-all-done.2 = bf16[128,4,128]{2,0,1:T(8,128)(2,1)S(1)} async-done(((bf16[128,4,128]{2,0,1:T(8,128)(2,1)}), bf16[128,4,128]{2,0,1:T(8,128)(2,1)S(1)}, u32[]{:S(2)}, u32[]{:S(2)}) %all-to-all-start.2) | async-done | bytes 131104 | tf_op jit(solution)/shard_map/all_to_all | solution.py:50
  23.1 3.6 %all-to-all-start.1 = ((bf16[128,32,128]{2,0,1:T(8,128)(2,1)}), bf16[128,32,128]{2,0,1:T(8,128)(2,1)S(1)}, u32[]{:S(2)}, u32[]{:S(2)}) async-start(bf16[128,32,128]{2,0,1:T(8,128)(2,1)} %copy.92), calls=%async_computation.1 | async-start | bytes 2097152 | tf_op jit(solution)/shard_map/all_to_all | solution.py:47
  28.6 2.0 %collective-permute-start.1 = (bf16[1,2,1,32,2,128]{5,3,4,1,0,2:T(8,128)(2,1)S(1)}, bf16[1,2,1,32,2,128]{5,3,4,1,0,2:T(8,128)(2,1)S(1)}, u32[]{:S(2)}, u32[]{:S(2)}) collective-permute-start(bf16[1,2,1,32,2,128]{5,3,4,1,0,2:T(8,128)(2,1)S(1)} %get-tuple-element.643), channel_id=1, source_target_pairs={{0,4},{2,6},{4,8},{6,10},{8,12},{10,14},{12,16},{14,18},{16,20},{1... | collective-permute-start | bytes 98312 | tf_op jit(solution)/shard_map/ppermute | solution.py:60
  30.6 2.5 %collective-permute-start.2 = (bf16[1,2,1,32,2,128]{5,3,4,1,0,2:T(8,128)(2,1)S(1)}, bf16[1,2,1,32,2,128]{5,3,4,1,0,2:T(8,128)(2,1)S(1)}, u32[]{:S(2)}, u32[]{:S(2)}) collective-permute-start(bf16[1,2,1,32,2,128]{5,3,4,1,0,2:T(8,128)(2,1)S(1)} %get-tuple-element.642), channel_id=1, source_target_pairs={{0,6},{2,8},{4,10},{6,12},{8,14},{10,16},{12,18},{14,20},{16,22},{... | collective-permute-start | bytes 98312 | tf_op jit(solution)/shard_map/ppermute | solution.py:60
  33.1 1.6 collective-permute-start.3
  34.8 1.3 collective-permute-start.5
  36.1 4.4 %collective-permute-start.6 = (bf16[1,2,1,32,2,128]{5,3,4,1,0,2:T(8,128)(2,1)S(1)}, bf16[1,2,1,32,2,128]{5,3,4,1,0,2:T(8,128)(2,1)S(1)}, u32[]{:S(2)}, u32[]{:S(2)}) collective-permute-start(bf16[1,2,1,32,2,128]{5,3,4,1,0,2:T(8,128)(2,1)S(1)} %get-tuple-element.638), channel_id=1, source_target_pairs={{0,14},{2,16},{4,18},{6,20},{8,22},{10,24},{12,26},{14,28},{16,30}... | collective-permute-start | bytes 98312 | tf_op jit(solution)/shard_map/ppermute | solution.py:60
  41.8 1.8 collective-permute-start.9
  43.6 2.9 %collective-permute-start.10 = (bf16[1,2,1,32,2,128]{5,3,4,1,0,2:T(8,128)(2,1)S(1)}, bf16[1,2,1,32,2,128]{5,3,4,1,0,2:T(8,128)(2,1)S(1)}, u32[]{:S(2)}, u32[]{:S(2)}) collective-permute-start(bf16[1,2,1,32,2,128]{5,3,4,1,0,2:T(8,128)(2,1)S(1)} %get-tuple-element.634), channel_id=1, source_target_pairs={{0,22},{2,24},{4,26},{6,28},{8,30},{10,0},{12,2},{14,4},{16,6},{18... | collective-permute-start | bytes 98312 | tf_op jit(solution)/shard_map/ppermute | solution.py:60
  46.6 1.9 collective-permute-start.11
  48.6 1.5 collective-permute-start.13
  50.1 2.3 %collective-permute-start.14 = (bf16[1,2,1,32,2,128]{5,3,4,1,0,2:T(8,128)(2,1)S(1)}, bf16[1,2,1,32,2,128]{5,3,4,1,0,2:T(8,128)(2,1)S(1)}, u32[]{:S(2)}, u32[]{:S(2)}) collective-permute-start(bf16[1,2,1,32,2,128]{5,3,4,1,0,2:T(8,128)(2,1)S(1)} %get-tuple-element.630), channel_id=1, source_target_pairs={{0,30},{2,0},{4,2},{6,4},{8,6},{10,8},{12,10},{14,12},{16,14},{18,... | collective-permute-start | bytes 98312 | tf_op jit(solution)/shard_map/ppermute | solution.py:60
  52.5 1.4 collective-permute-done.14
  55.3 4.4 %all-to-all-start.4 = ((bf16[128,32,128]{2,0,1:T(8,128)(2,1)}), bf16[128,32,128]{2,0,1:T(8,128)(2,1)}, u32[]{:S(2)}, u32[]{:S(2)}) async-start(bf16[128,32,128]{2,0,1:T(8,128)(2,1)} %copy.110), calls=%async_computation.4 | async-start | bytes 2097152 | tf_op jit(solution)/shard_map/all_to_all | solution.py:48
  59.7 0.7 copy.94
  60.4 1.8 fusion.57
  62.2 1.3 copy-done.8
  63.5 3.0 %copy.103 = f32[8,2,32,32,8]{3,4,2,1,0:T(8,128)} copy(f32[8,2,32,32,8]{3,2,4,1,0:T(8,128)S(1)} %fusion.57) | data formatting | bytes 1048576 | tf_op jit(solution)/shard_map/while | solution.py:107
  66.5 1.9 copy.107
  68.5 2.7 %fusion.97 = (f32[8,2,8,32]{3,2,1,0:T(8,128)S(1)}, f32[8,2,8,32,32]{3,4,2,1,0:T(8,128)S(1)}) fusion(bf16[8,32,2,8,128]{4,3,2,1,0:T(8,128)(2,1)S(1)} %bitcast.282, bf16[8,32,2,128,1]{3,1,0,2,4:T(8,128)(2,1)} %bitcast.289, pred[32,32]{0,1:T(8,128)(4,1)S(1)} %iota_compare_fusion), kind=kOutput, calls=%fused_computation.182 | convolution fusion | flops 33943552 | bytes 1721344 | tf_op jit(solution)/shard_map/pqkgd,pjkd->pkgqj/dot_general | solution.py:76
  71.2 1.3 copy-done.2
  73.2 4.2 %while.43 = (s32[]{:T(128)}, f32[8,2,8,32]{3,2,1,0:T(8,128)S(1)}, f32[8,2,8,32]{3,2,1,0:T(8,128)S(1)}, s32[]{:T(128)}, pred[8,1]{0,1:T(4,128)(4,1)S(1)}, /*index=5*/f32[8,2,32,32,8]{3,4,2,1,0:T(8,128)}, s32[]{:T(128)}) while((s32[]{:T(128)}, f32[8,2,8,32]{3,2,1,0:T(8,128)S(1)}, f32[8,2,8,32]{3,2,1,0:T(8,128)S(1)}, s32[]{:T(128)}, ...), condition=%wide.region_7.9_spmd, body=%wide.region_4.8_spmd.sunk | while | flops 925698 | bytes 3358841 | solution.py:107
  73.9 2.1 %bitcast_reduce_fusion.2 = f32[8,2,8,32]{3,2,1,0:T(8,128)S(1)} fusion(f32[8,2,32,32,8]{3,4,2,1,0:T(8,128)} %get-tuple-element.818, pred[8]{0:T(512)(128)(4,1)S(1)} %bitcast.308), kind=kLoop, calls=%fused_computation.4.clone.1 | loop fusion | flops 389120 | bytes 540680 | tf_op jit(solution)/shard_map/while/body/reduce_max | solution.py:101
  77.4 3.5 %convolution_bitcast_fusion.1 = f32[8,32,2,8,128]{4,1,3,2,0:T(8,128)} fusion(f32[8,2,8,32,32]{3,4,2,1,0:T(8,128)} %copy-done.2, f32[8,2,8,32]{3,2,1,0:T(8,128)S(1)} %log_add_fusion, bf16[8,32,2,128,1]{3,1,0,2,4:T(8,128)(2,1)S(1)} %bitcast.292), kind=kOutput, calls=%fused_computation.52 | convolution fusion | flops 33816576 | bytes 2768896 | tf_op jit(solution)/shard_map/pkgqj,pjkd->pqkgd/dot_general | solution.py:113
  81.0 4.8 %while.44 = (s32[]{:T(128)}, f32[8,32,2,8,128]{4,1,3,2,0:T(8,128)}, s32[]{:T(128)}, pred[8,1]{0,1:T(4,128)(4,1)S(1)}, f32[8,2,32,32,8]{2,3,4,1,0:T(8,128)S(1)}, ...) while((s32[]{:T(128)}, f32[8,32,2,8,128]{4,1,3,2,0:T(8,128)}, s32[]{:T(128)}, ...), condition=%wide.region_9.11_spmd, body=%wide.region_8.10_spmd.sunk | while | flops 34603008 | bytes 4866141 | solution.py:127
  81.9 3.3 %bitcast_add_fusion.6 = f32[8,32,2,8,128]{4,1,3,2,0:T(8,128)} fusion(f32[8,32,2,8,128]{4,1,3,2,0:T(8,128)} %get-tuple-element.829, f32[8,2,32,32,8]{2,3,4,1,0:T(8,128)S(1)} %get-tuple-element.840, f32[8,2,8,32]{3,2,1,0:T(8,128)S(1)} %get-tuple-element.841, pred[8]{0:T(512)(128)(4,1)S(1)} %bitcast.310, bf16[8,32,2,128]{3,1,2,0:T(8,128)(2,1)S(1)} %get-tuple-element.842), kind=kOutput, calls=%fused_computation.9.clone.1 | convolution fusion | flops 34603008 | bytes 4866056 | tf_op jit(solution)/shard_map/while/body/pkgqj,pjkd->pqkgd/dot_general | solution.py:123
  85.8 1.9 copy.112
  87.8 3.2 %fusion.52 = f32[8,2,32,32,8]{3,2,4,1,0:T(8,128)} fusion(bf16[8,32,2,8,128]{4,3,2,1,0:T(8,128)(2,1)S(1)} %bitcast.276, bf16[8,32,2,128]{3,1,2,0:T(8,128)(2,1)S(1)} %get-tuple-element.883), kind=kOutput, calls=%fused_computation.76 | convolution fusion | flops 33554432 | bytes 1703936 | tf_op jit(solution)/shard_map/while/body/pqkgd,pjkd->pkgqj/dot_general | solution.py:137
  90.9 3.2 %multiply_reduce_fusion = (f32[8,32,2,8]{3,2,1,0:T(2,128)}, bf16[8,32,2,8,128]{4,3,2,1,0:T(8,128)(2,1)}) fusion(bf16[8,32,2,8,128]{4,3,2,1,0:T(8,128)(2,1)S(1)} %bitcast.277, f32[8,32,2,8,128]{4,1,3,2,0:T(8,128)S(1)} %copy-done.1), kind=kLoop, calls=%fused_computation.47 | loop fusion | flops 2093056 | bytes 4210688 | tf_op jit(solution)/shard_map/reduce_sum | solution.py:130
  94.1 1.0 copy.115
  95.2 3.3 %convolution_bitcast_fusion.4 = f32[1,8,32,2,128]{4,2,3,1,0:T(8,128)} fusion(f32[8,2,32,32,8]{3,2,4,1,0:T(8,128)} %copy-done.8, f32[8,2,8,32]{3,2,1,0:T(8,128)S(1)} %get-tuple-element.881, pred[8]{0:T(512)(128)(4,1)S(1)} %get-tuple-element.627, bf16[8,32,2,8,128]{4,3,2,1,0:T(8,128)(2,1)S(1)} %bitcast.278), kind=kOutput, calls=%fused_computation.56 | convolution fusion | flops 34078720 | bytes 1851400 | tf_op jit(solution)/shard_map/while/body/pkgqj,pqkgd->pjkd/dot_general | solution.py:148
  98.5 2.8 %fusion.28 = bf16[8,2,8,32,32]{3,4,2,1,0:T(8,128)(2,1)} fusion(f32[8,2,8,32,32]{3,4,2,1,0:T(8,128)S(1)} %copy-done.3, f32[8,2,8,32]{3,2,1,0:T(8,128)S(1)} %copy.115, f32[8,2,8,32]{3,2,1,0:T(8,128)S(1)} %get-tuple-element.881, bf16[8,32,2,8,128]{4,3,2,1,0:T(8,128)(2,1)S(1)} %bitcast.279, bf16[8,32,2,128,1]{3,1,0,2,4:T(8,128)(2,1)S(1)} %bitcast.293), kind=kOutput, calls=%fused_computation.42 | convolution fusion | flops 34078720 | bytes 1998848 | tf_op jit(solution)/shard_map/pqkgd,pjkd->pkgqj/dot_general | solution.py:137
  101.3 1.0 fusion.33
  102.3 3.0 %copy.123 = f32[8,2,32,32,8]{2,3,4,1,0:T(8,128)} copy(f32[8,2,32,32,8]{3,2,4,1,0:T(8,128)} %fusion.52) | data formatting | bytes 1048576 | tf_op jit(solution)/shard_map/while | solution.py:173
  105.3 0.9 fusion.60
  106.2 1.5 copy.125
  107.7 1.9 convolution_bitcast_fusion
  110.0 6.4 %while.45 = (s32[]{:T(128)}, f32[8,32,2,8,128]{4,1,3,2,0:T(8,128)}, f32[2,16,32,2,128]{4,3,2,1,0:T(2,128)S(1)}, s32[]{:T(128)}, pred[8,1]{0,1:T(4,128)(4,1)S(1)}...) while((s32[]{:T(128)}, f32[8,32,2,8,128]{4,1,3,2,0:T(8,128)}, ...), condition=%wide.region_12.14_spmd, body=%wide.region_11.13_spmd.sunk | while | flops 35127296 | bytes 12746905 | solution.py:173
  110.7 4.1 %bitcast_add_fusion.7 = f32[8,32,2,8,128]{4,1,3,2,0:T(8,128)} fusion(f32[8,32,2,8,128]{4,1,3,2,0:T(8,128)} %get-tuple-element.857, f32[8,2,32,32,8]{2,3,4,1,0:T(8,128)} %get-tuple-element.875, f32[8,2,32,32,8]{2,3,4,1,0:T(8,128)S(1)} %get-tuple-element.873, f32[8,2,8,32]{3,2,1,0:T(8,128)S(1)} %get-tuple-element.876, ...), kind=kOutput, calls=%fused_computation.20.clone.1 | convolution fusion | flops 34865152 | bytes 5406728 | tf_op jit(solution)/shard_map/while/body/pkgqj,pjkd->pqkgd/dot_general | solution.py:141
  116.4 3.9 %fusion.29 = bf16[8,32,2,8,128]{4,3,2,1,0:T(8,128)(2,1)} fusion(f32[8,32,2,8,128]{4,1,3,2,0:T(8,128)} %get-tuple-element.466), kind=kLoop, calls=%fused_computation.45 | loop fusion | flops 1048576 | bytes 3145728 | tf_op jit(solution)/shard_map/convert_element_type | solution.py:183
  120.4 3.6 %all-to-all-start.5 = ((bf16[256,16,128]{2,1,0:T(8,128)(2,1)}), bf16[256,16,128]{2,1,0:T(8,128)(2,1)S(1)}, u32[]{:S(2)}, u32[]{:S(2)}) async-start(bf16[256,16,128]{2,1,0:T(8,128)(2,1)} %bitcast.87), calls=%async_computation.5 | async-start | bytes 2097152 | tf_op jit(solution)/shard_map/all_to_all | solution.py:187
  124.0 14.9 %all-to-all-done.5 = bf16[256,16,128]{2,1,0:T(8,128)(2,1)S(1)} async-done(((bf16[256,16,128]{2,1,0:T(8,128)(2,1)}), bf16[256,16,128]{2,1,0:T(8,128)(2,1)S(1)}, u32[]{:S(2)}, u32[]{:S(2)}) %all-to-all-start.5) | async-done | bytes 1048608 | tf_op jit(solution)/shard_map/all_to_all | solution.py:187
  138.9 28.3 %all_to_all.119 = f32[2,16,32,2,128]{4,3,2,0,1:T(2,128)} all-to-all(f32[2,16,32,2,128]{4,3,2,0,1:T(2,128)S(1)} %copy.129), channel_id=1, replica_groups=mesh['grp'=16,'uly'=2] {'grp'}, dimensions={1} | all-to-all | bytes 2097152 | tf_op jit(solution)/shard_map/all_to_all | solution.py:177
  167.2 4.7 %all-to-all-start.3 = ((bf16[256,16,128]{2,1,0:T(8,128)(2,1)}), bf16[256,16,128]{2,1,0:T(8,128)(2,1)}, u32[]{:S(2)}, u32[]{:S(2)}) async-start(bf16[256,16,128]{2,1,0:T(8,128)(2,1)} %bitcast.285), calls=%async_computation.3 | async-start | bytes 2097152 | tf_op jit(solution)/shard_map/all_to_all | solution.py:186
  171.9 2.2 %fusion.39 = f32[2,32,2,128,8]{3,4,2,1,0:T(8,128)S(1)} fusion(f32[2,16,32,2,128]{4,3,2,0,1:T(2,128)} %all_to_all.119, s32[16]{0:T(128)S(1)} %fusion.72, pred[16]{0:T(512)(128)(4,1)S(1)} %get-tuple-element.620), kind=kOutput, calls=%fused_computation.64 | convolution fusion | flops 25166080 | bytes 1572944 | tf_op jit(solution)/shard_map/sp,xsjkd->xpjkd/dot_general | solution.py:178
  175.2 0.8 copy.138
  176.0 10.9 %all-to-all-done.3 = bf16[256,16,128]{2,1,0:T(8,128)(2,1)} async-done(((bf16[256,16,128]{2,1,0:T(8,128)(2,1)}), bf16[256,16,128]{2,1,0:T(8,128)(2,1)}, u32[]{:S(2)}, u32[]{:S(2)}) %all-to-all-start.3) | async-done | bytes 1048608 | tf_op jit(solution)/shard_map/all_to_all | solution.py:186
  186.8 3.4 %all-to-all-start.8 = ((bf16[256,2,128]{2,1,0:T(2,128)(2,1)}), bf16[256,2,128]{2,1,0:T(2,128)(2,1)S(1)}, u32[]{:S(2)}, u32[]{:S(2)}) async-start(bf16[256,2,128]{2,1,0:T(2,128)(2,1)} %copy.138), calls=%async_computation.8 | async-start | bytes 262144 | tf_op jit(solution)/shard_map/all_to_all | solution.py:191
  190.2 2.1 %fusion.36 = bf16[8,32,2,128]{3,1,2,0:T(8,128)(2,1)S(1)} fusion(bf16[8,2,8,32,32]{3,4,2,1,0:T(8,128)(2,1)} %fusion.28, bf16[8,32,2,8,128]{4,3,2,1,0:T(8,128)(2,1)} %bitcast.283, f32[2,8,32,2,128]{4,2,3,1,0:T(8,128)} %bitcast.296), kind=kOutput, calls=%fused_computation.62 | convolution fusion | flops 33751040 | bytes 1703936 | tf_op jit(solution)/shard_map/pkgqj,pqkgd->pjkd/dot_general | solution.py:145
  192.3 0.8 copy.133
  193.1 1.6 all-to-all-done.8
  194.7 3.4 %all-to-all-start.7 = ((bf16[256,2,128]{2,1,0:T(2,128)(2,1)}), bf16[256,2,128]{2,1,0:T(2,128)(2,1)S(1)}, u32[]{:S(2)}, u32[]{:S(2)}) async-start(bf16[256,2,128]{2,1,0:T(2,128)(2,1)} %copy.133), calls=%async_computation.7 | async-start | bytes 262144 | tf_op jit(solution)/shard_map/all_to_all | solution.py:190
  198.1 1.2 copy.127
  199.2 2.4 %copy.109 = bf16[128,2,16,128]{3,2,1,0:T(8,128)(2,1)} copy(bf16[128,2,16,128]{3,2,0,1:T(8,128)(2,1)} %bitcast.62) | data formatting | bytes 2097152 | tf_op jit(solution)/shard_map/all_to_all | solution.py:186
  201.6 0.8 copy.142
  202.6 0.8 copy.141
  (130 shorter events, 10.4 us)
Async XLA Ops:
  0.6 10.9 %copy-start.22 = (bf16[128,32,128]{2,1,0:T(8,128)(2,1)S(1)}, bf16[128,32,128]{2,1,0:T(8,128)(2,1)}, u32[]{:S(2)}) copy-start(bf16[128,32,128]{2,1,0:T(8,128)(2,1)} %param.14) | copy-start | bytes 3145732
  0.6 12.3 %copy-start.23 = (bf16[128,32,128]{2,1,0:T(8,128)(2,1)S(1)}, bf16[128,32,128]{2,1,0:T(8,128)(2,1)}, u32[]{:S(2)}) copy-start(bf16[128,32,128]{2,1,0:T(8,128)(2,1)} %param.17) | copy-start | bytes 3145732
  2.4 12.6 %all-to-all-start = ((bf16[128,4,128]{2,0,1:T(8,128)(2,1)}), bf16[128,4,128]{2,0,1:T(8,128)(2,1)S(1)}, u32[]{:S(2)}, u32[]{:S(2)}) async-start(bf16[128,4,128]{2,0,1:T(8,128)(2,1)} %copy.90), calls=%async_computation | async-start | bytes 262144 | tf_op jit(solution)/shard_map/all_to_all | solution.py:49
  15.0 8.1 %all-to-all-start.2 = ((bf16[128,4,128]{2,0,1:T(8,128)(2,1)}), bf16[128,4,128]{2,0,1:T(8,128)(2,1)S(1)}, u32[]{:S(2)}, u32[]{:S(2)}) async-start(bf16[128,4,128]{2,0,1:T(8,128)(2,1)} %copy.98), calls=%async_computation.2 | async-start | bytes 262144 | tf_op jit(solution)/shard_map/all_to_all | solution.py:50
  18.6 8.2 %copy-start.16 = (bf16[2,128,2,128]{3,1,0,2:T(8,128)(2,1)}, bf16[2,128,2,128]{3,1,0,2:T(8,128)(2,1)S(1)}, u32[]{:S(2)}) copy-start(bf16[2,128,2,128]{3,1,0,2:T(8,128)(2,1)S(1)} %copy.91) | copy-start | bytes 393220
  23.1 32.1 %all-to-all-start.1 = ((bf16[128,32,128]{2,0,1:T(8,128)(2,1)}), bf16[128,32,128]{2,0,1:T(8,128)(2,1)S(1)}, u32[]{:S(2)}, u32[]{:S(2)}) async-start(bf16[128,32,128]{2,0,1:T(8,128)(2,1)} %copy.92), calls=%async_computation.1 | async-start | bytes 2097152 | tf_op jit(solution)/shard_map/all_to_all | solution.py:47
  26.7 0.7 copy-start.18
  28.4 6.4 %collective-permute-start = (bf16[1,2,1,32,2,128]{5,3,4,1,0,2:T(8,128)(2,1)S(1)}, bf16[1,2,1,32,2,128]{5,3,4,1,0,2:T(8,128)(2,1)S(1)}, u32[]{:S(2)}, u32[]{:S(2)}) collective-permute-start(bf16[1,2,1,32,2,128]{5,3,4,1,0,2:T(8,128)(2,1)S(1)} %get-tuple-element.644), channel_id=1, source_target_pairs={{0,2},{2,4},{4,6},{6,8},{8,10},{10,12},{12,14},{14,16},{16,18},{18... | collective-permute-start | bytes 98312 | tf_op jit(solution)/shard_map/ppermute | solution.py:60
  28.6 7.5 %collective-permute-start.1 = (bf16[1,2,1,32,2,128]{5,3,4,1,0,2:T(8,128)(2,1)S(1)}, bf16[1,2,1,32,2,128]{5,3,4,1,0,2:T(8,128)(2,1)S(1)}, u32[]{:S(2)}, u32[]{:S(2)}) collective-permute-start(bf16[1,2,1,32,2,128]{5,3,4,1,0,2:T(8,128)(2,1)S(1)} %get-tuple-element.643), channel_id=1, source_target_pairs={{0,4},{2,6},{4,8},{6,10},{8,12},{10,14},{12,16},{14,18},{16,20},{1... | collective-permute-start | bytes 98312 | tf_op jit(solution)/shard_map/ppermute | solution.py:60
  30.6 9.8 %collective-permute-start.2 = (bf16[1,2,1,32,2,128]{5,3,4,1,0,2:T(8,128)(2,1)S(1)}, bf16[1,2,1,32,2,128]{5,3,4,1,0,2:T(8,128)(2,1)S(1)}, u32[]{:S(2)}, u32[]{:S(2)}) collective-permute-start(bf16[1,2,1,32,2,128]{5,3,4,1,0,2:T(8,128)(2,1)S(1)} %get-tuple-element.642), channel_id=1, source_target_pairs={{0,6},{2,8},{4,10},{6,12},{8,14},{10,16},{12,18},{14,20},{16,22},{... | collective-permute-start | bytes 98312 | tf_op jit(solution)/shard_map/ppermute | solution.py:60
  33.1 7.8 %collective-permute-start.3 = (bf16[1,2,1,32,2,128]{5,3,4,1,0,2:T(8,128)(2,1)S(1)}, bf16[1,2,1,32,2,128]{5,3,4,1,0,2:T(8,128)(2,1)S(1)}, u32[]{:S(2)}, u32[]{:S(2)}) collective-permute-start(bf16[1,2,1,32,2,128]{5,3,4,1,0,2:T(8,128)(2,1)S(1)} %get-tuple-element.641), channel_id=1, source_target_pairs={{0,8},{2,10},{4,12},{6,14},{8,16},{10,18},{12,20},{14,22},{16,24},... | collective-permute-start | bytes 98312 | tf_op jit(solution)/shard_map/ppermute | solution.py:60
  34.7 7.2 %collective-permute-start.4 = (bf16[1,2,1,32,2,128]{5,3,4,1,0,2:T(8,128)(2,1)S(1)}, bf16[1,2,1,32,2,128]{5,3,4,1,0,2:T(8,128)(2,1)S(1)}, u32[]{:S(2)}, u32[]{:S(2)}) collective-permute-start(bf16[1,2,1,32,2,128]{5,3,4,1,0,2:T(8,128)(2,1)S(1)} %get-tuple-element.640), channel_id=1, source_target_pairs={{0,10},{2,12},{4,14},{6,16},{8,18},{10,20},{12,22},{14,24},{16,26}... | collective-permute-start | bytes 98312 | tf_op jit(solution)/shard_map/ppermute | solution.py:60
  34.8 8.9 %collective-permute-start.5 = (bf16[1,2,1,32,2,128]{5,3,4,1,0,2:T(8,128)(2,1)S(1)}, bf16[1,2,1,32,2,128]{5,3,4,1,0,2:T(8,128)(2,1)S(1)}, u32[]{:S(2)}, u32[]{:S(2)}) collective-permute-start(bf16[1,2,1,32,2,128]{5,3,4,1,0,2:T(8,128)(2,1)S(1)} %get-tuple-element.639), channel_id=1, source_target_pairs={{0,12},{2,14},{4,16},{6,18},{8,20},{10,22},{12,24},{14,26},{16,28}... | collective-permute-start | bytes 98312 | tf_op jit(solution)/shard_map/ppermute | solution.py:60
  36.1 10.5 %collective-permute-start.6 = (bf16[1,2,1,32,2,128]{5,3,4,1,0,2:T(8,128)(2,1)S(1)}, bf16[1,2,1,32,2,128]{5,3,4,1,0,2:T(8,128)(2,1)S(1)}, u32[]{:S(2)}, u32[]{:S(2)}) collective-permute-start(bf16[1,2,1,32,2,128]{5,3,4,1,0,2:T(8,128)(2,1)S(1)} %get-tuple-element.638), channel_id=1, source_target_pairs={{0,14},{2,16},{4,18},{6,20},{8,22},{10,24},{12,26},{14,28},{16,30}... | collective-permute-start | bytes 98312 | tf_op jit(solution)/shard_map/ppermute | solution.py:60
  40.4 8.0 %collective-permute-start.7 = (bf16[1,2,1,32,2,128]{5,3,4,1,0,2:T(8,128)(2,1)S(1)}, bf16[1,2,1,32,2,128]{5,3,4,1,0,2:T(8,128)(2,1)S(1)}, u32[]{:S(2)}, u32[]{:S(2)}) collective-permute-start(bf16[1,2,1,32,2,128]{5,3,4,1,0,2:T(8,128)(2,1)S(1)} %get-tuple-element.637), channel_id=1, source_target_pairs={{0,16},{2,18},{4,20},{6,22},{8,24},{10,26},{12,28},{14,30},{16,0},... | collective-permute-start | bytes 98312 | tf_op jit(solution)/shard_map/ppermute | solution.py:60
  40.9 7.7 %collective-permute-start.8 = (bf16[1,2,1,32,2,128]{5,3,4,1,0,2:T(8,128)(2,1)S(1)}, bf16[1,2,1,32,2,128]{5,3,4,1,0,2:T(8,128)(2,1)S(1)}, u32[]{:S(2)}, u32[]{:S(2)}) collective-permute-start(bf16[1,2,1,32,2,128]{5,3,4,1,0,2:T(8,128)(2,1)S(1)} %get-tuple-element.636), channel_id=1, source_target_pairs={{0,18},{2,20},{4,22},{6,24},{8,26},{10,28},{12,30},{14,0},{16,2},{... | collective-permute-start | bytes 98312 | tf_op jit(solution)/shard_map/ppermute | solution.py:60
  41.8 8.2 %collective-permute-start.9 = (bf16[1,2,1,32,2,128]{5,3,4,1,0,2:T(8,128)(2,1)S(1)}, bf16[1,2,1,32,2,128]{5,3,4,1,0,2:T(8,128)(2,1)S(1)}, u32[]{:S(2)}, u32[]{:S(2)}) collective-permute-start(bf16[1,2,1,32,2,128]{5,3,4,1,0,2:T(8,128)(2,1)S(1)} %get-tuple-element.635), channel_id=1, source_target_pairs={{0,20},{2,22},{4,24},{6,26},{8,28},{10,30},{12,0},{14,2},{16,4},{1... | collective-permute-start | bytes 98312 | tf_op jit(solution)/shard_map/ppermute | solution.py:60
  43.6 8.7 %collective-permute-start.10 = (bf16[1,2,1,32,2,128]{5,3,4,1,0,2:T(8,128)(2,1)S(1)}, bf16[1,2,1,32,2,128]{5,3,4,1,0,2:T(8,128)(2,1)S(1)}, u32[]{:S(2)}, u32[]{:S(2)}) collective-permute-start(bf16[1,2,1,32,2,128]{5,3,4,1,0,2:T(8,128)(2,1)S(1)} %get-tuple-element.634), channel_id=1, source_target_pairs={{0,22},{2,24},{4,26},{6,28},{8,30},{10,0},{12,2},{14,4},{16,6},{18... | collective-permute-start | bytes 98312 | tf_op jit(solution)/shard_map/ppermute | solution.py:60
  46.6 5.8 %collective-permute-start.11 = (bf16[1,2,1,32,2,128]{5,3,4,1,0,2:T(8,128)(2,1)S(1)}, bf16[1,2,1,32,2,128]{5,3,4,1,0,2:T(8,128)(2,1)S(1)}, u32[]{:S(2)}, u32[]{:S(2)}) collective-permute-start(bf16[1,2,1,32,2,128]{5,3,4,1,0,2:T(8,128)(2,1)S(1)} %get-tuple-element.633), channel_id=1, source_target_pairs={{0,24},{2,26},{4,28},{6,30},{8,0},{10,2},{12,4},{14,6},{16,8},{18,... | collective-permute-start | bytes 98312 | tf_op jit(solution)/shard_map/ppermute | solution.py:60
  48.5 3.9 %collective-permute-start.12 = (bf16[1,2,1,32,2,128]{5,3,4,1,0,2:T(8,128)(2,1)S(1)}, bf16[1,2,1,32,2,128]{5,3,4,1,0,2:T(8,128)(2,1)S(1)}, u32[]{:S(2)}, u32[]{:S(2)}) collective-permute-start(bf16[1,2,1,32,2,128]{5,3,4,1,0,2:T(8,128)(2,1)S(1)} %get-tuple-element.632), channel_id=1, source_target_pairs={{0,26},{2,28},{4,30},{6,0},{8,2},{10,4},{12,6},{14,8},{16,10},{18,... | collective-permute-start | bytes 98312 | tf_op jit(solution)/shard_map/ppermute | solution.py:60
  48.6 4.0 %collective-permute-start.13 = (bf16[1,2,1,32,2,128]{5,3,4,1,0,2:T(8,128)(2,1)S(1)}, bf16[1,2,1,32,2,128]{5,3,4,1,0,2:T(8,128)(2,1)S(1)}, u32[]{:S(2)}, u32[]{:S(2)}) collective-permute-start(bf16[1,2,1,32,2,128]{5,3,4,1,0,2:T(8,128)(2,1)S(1)} %get-tuple-element.631), channel_id=1, source_target_pairs={{0,28},{2,30},{4,0},{6,2},{8,4},{10,6},{12,8},{14,10},{16,12},{18,... | collective-permute-start | bytes 98312 | tf_op jit(solution)/shard_map/ppermute | solution.py:60
  50.1 3.9 %collective-permute-start.14 = (bf16[1,2,1,32,2,128]{5,3,4,1,0,2:T(8,128)(2,1)S(1)}, bf16[1,2,1,32,2,128]{5,3,4,1,0,2:T(8,128)(2,1)S(1)}, u32[]{:S(2)}, u32[]{:S(2)}) collective-permute-start(bf16[1,2,1,32,2,128]{5,3,4,1,0,2:T(8,128)(2,1)S(1)} %get-tuple-element.630), channel_id=1, source_target_pairs={{0,30},{2,0},{4,2},{6,4},{8,6},{10,8},{12,10},{14,12},{16,14},{18,... | collective-permute-start | bytes 98312 | tf_op jit(solution)/shard_map/ppermute | solution.py:60
  55.3 30.6 %all-to-all-start.4 = ((bf16[128,32,128]{2,0,1:T(8,128)(2,1)}), bf16[128,32,128]{2,0,1:T(8,128)(2,1)}, u32[]{:S(2)}, u32[]{:S(2)}) async-start(bf16[128,32,128]{2,0,1:T(8,128)(2,1)} %copy.110), calls=%async_computation.4 | async-start | bytes 2097152 | tf_op jit(solution)/shard_map/all_to_all | solution.py:48
  60.4 8.1 %copy-start.10 = (bf16[2,128,16,128]{3,2,1,0:T(8,128)(2,1)}, bf16[2,128,16,128]{3,2,1,0:T(8,128)(2,1)S(1)}, u32[]{:S(2)}) copy-start(bf16[2,128,16,128]{3,2,1,0:T(8,128)(2,1)S(1)} %copy.94) | copy-start | bytes 3145732
  62.1 1.4 copy-start.8
  71.2 1.4 copy-start.2
  73.2 4.3 %copy-start.19 = (bf16[2,128,2,128]{3,1,0,2:T(8,128)(2,1)S(1)}, bf16[2,128,2,128]{3,1,0,2:T(8,128)(2,1)}, u32[]{:S(2)}) copy-start(bf16[2,128,2,128]{3,1,0,2:T(8,128)(2,1)} %copy-done.18) | copy-start | bytes 393220
  73.9 2.2 %copy-start = (f32[8,2,32,32,8]{3,4,2,1,0:T(8,128)S(1)}, f32[8,2,32,32,8]{3,4,2,1,0:T(8,128)}, u32[]{:S(2)}) copy-start(f32[8,2,32,32,8]{3,4,2,1,0:T(8,128)} %get-tuple-element.818) | copy-start | bytes 1572868 | tf_op jit(solution)/shard_map/while
  87.7 10.7 %copy-start.6 = (bf16[2,128,16,128]{3,2,1,0:T(8,128)(2,1)}, bf16[2,128,16,128]{3,2,1,0:T(8,128)(2,1)S(1)}, u32[]{:S(2)}) copy-start(bf16[2,128,16,128]{3,2,1,0:T(8,128)(2,1)S(1)} %copy.112) | copy-start | bytes 3145732
  87.7 3.2 %copy-start.1 = (f32[8,32,2,8,128]{4,1,3,2,0:T(8,128)S(1)}, f32[8,32,2,8,128]{4,1,3,2,0:T(8,128)}, u32[]{:S(2)}) copy-start(f32[8,32,2,8,128]{4,1,3,2,0:T(8,128)} %get-tuple-element.465) | copy-start | bytes 6291460
  95.2 3.3 %copy-start.3 = (f32[8,2,8,32,32]{3,4,2,1,0:T(8,128)S(1)}, f32[8,2,8,32,32]{3,4,2,1,0:T(8,128)}, u32[]{:S(2)}) copy-start(f32[8,2,8,32,32]{3,4,2,1,0:T(8,128)} %copy-done.2) | copy-start | bytes 1572868
  95.2 3.3 %copy-start.20 = (bf16[2,128,2,128]{3,1,0,2:T(8,128)(2,1)S(1)}, bf16[2,128,2,128]{3,1,0,2:T(8,128)(2,1)}, u32[]{:S(2)}) copy-start(bf16[2,128,2,128]{3,1,0,2:T(8,128)(2,1)} %copy-done.18) | copy-start | bytes 393220
  95.2 6.1 %copy-start.12 = (f32[8,2,32,32,8]{3,2,4,1,0:T(8,128)S(1)}, f32[8,2,32,32,8]{3,2,4,1,0:T(8,128)}, u32[]{:S(2)}) copy-start(f32[8,2,32,32,8]{3,2,4,1,0:T(8,128)} %fusion.52) | copy-start | bytes 1572868
  98.5 2.8 %copy-start.9 = (f32[8,2,32,32,8]{3,2,4,1,0:T(8,128)S(1)}, f32[8,2,32,32,8]{3,2,4,1,0:T(8,128)}, u32[]{:S(2)}) copy-start(f32[8,2,32,32,8]{3,2,4,1,0:T(8,128)} %copy-done.8) | copy-start | bytes 1572868
  98.5 2.8 %copy-start.11 = (bf16[2,128,16,128]{3,2,1,0:T(8,128)(2,1)S(1)}, bf16[2,128,16,128]{3,2,1,0:T(8,128)(2,1)}, u32[]{:S(2)}) copy-start(bf16[2,128,16,128]{3,2,1,0:T(8,128)(2,1)} %copy-done.10) | copy-start | bytes 3145732
  102.3 3.0 %copy-start.24 = (f32[1,8,32,2,128]{4,2,3,1,0:T(8,128)S(1)}, f32[1,8,32,2,128]{4,2,3,1,0:T(8,128)}, u32[]{:S(2)}) copy-start(f32[1,8,32,2,128]{4,2,3,1,0:T(8,128)} %convolution_bitcast_fusion.4) | copy-start | bytes 786436
  105.3 2.4 %copy-start.13 = (bf16[8,2,8,32,32]{3,4,2,1,0:T(8,128)(2,1)S(1)}, bf16[8,2,8,32,32]{3,4,2,1,0:T(8,128)(2,1)}, u32[]{:S(2)}) copy-start(bf16[8,2,8,32,32]{3,4,2,1,0:T(8,128)(2,1)} %fusion.28) | copy-start | bytes 786436
  105.3 2.4 %copy-start.17 = (bf16[2,128,2,128]{3,1,0,2:T(8,128)(2,1)S(1)}, bf16[2,128,2,128]{3,1,0,2:T(8,128)(2,1)}, u32[]{:S(2)}) copy-start(bf16[2,128,2,128]{3,1,0,2:T(8,128)(2,1)} %copy-done.16) | copy-start | bytes 393220
  110.7 4.1 %copy-start.5 = (f32[2,32,2,128,16]{3,2,1,4,0:T(2,128)S(1)}, f32[2,32,2,128,16]{3,2,1,4,0:T(2,128)}, u32[]{:S(2)}) copy-start(f32[2,32,2,128,16]{3,2,1,4,0:T(2,128)} %get-tuple-element.878) | copy-start | bytes 3145732 | tf_op jit(solution)/shard_map/while
  120.4 18.6 %all-to-all-start.5 = ((bf16[256,16,128]{2,1,0:T(8,128)(2,1)}), bf16[256,16,128]{2,1,0:T(8,128)(2,1)S(1)}, u32[]{:S(2)}, u32[]{:S(2)}) async-start(bf16[256,16,128]{2,1,0:T(8,128)(2,1)} %bitcast.87), calls=%async_computation.5 | async-start | bytes 2097152 | tf_op jit(solution)/shard_map/all_to_all | solution.py:187
  138.9 28.3 %copy-start.14 = (bf16[256,16,128]{2,1,0:T(8,128)(2,1)}, bf16[256,16,128]{2,1,0:T(8,128)(2,1)S(1)}, u32[]{:S(2)}) copy-start(bf16[256,16,128]{2,1,0:T(8,128)(2,1)S(1)} %all-to-all-done.5) | copy-start | bytes 3145732
  167.2 7.1 %copy-start.4 = (f32[8,2,8,32,32]{3,4,2,1,0:T(8,128)S(1)}, f32[8,2,8,32,32]{3,4,2,1,0:T(8,128)}, u32[]{:S(2)}) copy-start(f32[8,2,8,32,32]{3,4,2,1,0:T(8,128)} %copy-done.2) | copy-start | bytes 1572868
  167.2 7.1 %copy-start.7 = (bf16[2,128,16,128]{3,2,1,0:T(8,128)(2,1)S(1)}, bf16[2,128,16,128]{3,2,1,0:T(8,128)(2,1)}, u32[]{:S(2)}) copy-start(bf16[2,128,16,128]{3,2,1,0:T(8,128)(2,1)} %copy-done.6) | copy-start | bytes 3145732
  167.2 19.6 %all-to-all-start.3 = ((bf16[256,16,128]{2,1,0:T(8,128)(2,1)}), bf16[256,16,128]{2,1,0:T(8,128)(2,1)}, u32[]{:S(2)}, u32[]{:S(2)}) async-start(bf16[256,16,128]{2,1,0:T(8,128)(2,1)} %bitcast.285), calls=%async_computation.3 | async-start | bytes 2097152 | tf_op jit(solution)/shard_map/all_to_all | solution.py:186
  174.3 0.8 copy-start.21
  175.2 22.9 %copy-start.15 = (bf16[256,16,128]{2,1,0:T(8,128)(2,1)S(1)}, bf16[256,16,128]{2,1,0:T(8,128)(2,1)}, u32[]{:S(2)}) copy-start(bf16[256,16,128]{2,1,0:T(8,128)(2,1)} %copy-done.14) | copy-start | bytes 3145732
  186.8 7.8 %all-to-all-start.8 = ((bf16[256,2,128]{2,1,0:T(2,128)(2,1)}), bf16[256,2,128]{2,1,0:T(2,128)(2,1)S(1)}, u32[]{:S(2)}, u32[]{:S(2)}) async-start(bf16[256,2,128]{2,1,0:T(2,128)(2,1)} %copy.138), calls=%async_computation.8 | async-start | bytes 262144 | tf_op jit(solution)/shard_map/all_to_all | solution.py:191
  194.7 7.8 %all-to-all-start.7 = ((bf16[256,2,128]{2,1,0:T(2,128)(2,1)}), bf16[256,2,128]{2,1,0:T(2,128)(2,1)S(1)}, u32[]{:S(2)}, u32[]{:S(2)}) async-start(bf16[256,2,128]{2,1,0:T(2,128)(2,1)} %copy.133), calls=%async_computation.7 | async-start | bytes 262144 | tf_op jit(solution)/shard_map/all_to_all | solution.py:190
